TPU v7x, 32 devices: a whole 2x2x4 slice. The times are simulated.
32 devices in a mesh: patch: 2 (over x), epoch: 16 (over z, y, core).
Axes of the slice: x: 2, y: 2, z: 4, core: 2. Of those that a mesh axis runs over, the one named last changes fastest.
Arguments:
- images: float32 [32, 128, 1024], P(('patch', 'epoch')), parts along dimension 0, may hold values from -20 to 20, as said below
- variance: float32 [32], P(('patch', 'epoch')), parts along dimension 0, may hold values from 0.25 to 4
- zero_point: float32 [32], P(('patch', 'epoch')), parts along dimension 0, may hold values from 0.5 to 2
- block_mask: int32 [32, 1], P(('patch', 'epoch')), parts along dimension 0, may hold values 0 or 1
- stamps: int32 [32, 512], P(('patch', 'epoch')), parts along dimension 0, may hold values from 0 to 131071
- owners: int32 [8], P('patch'), parts along dimension 0, may hold values from 0 to 15
Outputs:
- significance: float32 [32, 128, 1024], P(('patch', 'epoch')), parts along dimension 0
- coefficients: float32 [32, 15], P(('patch', 'epoch')), parts along dimension 0
There are 2 independent parts, one for each index of `patch`. A program takes and returns all parts, laid end to end along the dimension named above; each array names one. Nothing has to cross between parts.
Inputs may be any that keep to these rules, and one draw needn't show every extreme that they name: `images`: each epoch is a common sky times an epoch scale plus noise.
All inputs are finite; a program needn't handle non-finite values. No bound on the sum of `block_mask` on one device may be relied on, other than what follows from the above.
Results may differ from a plain program's by a relative error of at most 0.00075.
The roundings to bfloat16 on the way count: a program that leaves them out, or rounds other values in their place, can miss the bound.
Values sent between devices are 32-bit elements; how exact they have to be, the bound alone decides.
A program may use at most 64 MiB of HBM per device.

v0:
```python
import functools
import math

import jax
import jax.numpy as jnp
from jax import lax
from jax.experimental import pallas as pl
from jax.experimental.pallas import tpu as pltpu
from jax.sharding import PartitionSpec as P

TILES = 4
KHALF = 7
NBASIS = 12
LANES = 128

sigma_list = (0.75, 1.5, 3.0)
basis_pairs = ((0, 0), (2, 0), (0, 2), (1, 1))
MESH = pl.DeviceIdType.MESH


def tap_values(offset, sigma, degree):
    scaled = offset / sigma
    power = jnp.ones_like(scaled)
    for _ in range(degree):
        power = power * scaled
    value = jnp.exp(-0.5 * scaled * scaled) * power / (math.sqrt(2.0 * math.pi) * sigma)
    return jnp.where(jnp.abs(offset) <= KHALF, value, 0.0).astype(jnp.bfloat16)


def grid_of(count):
    chips = count // 2
    middle = 1
    while middle * 2 * middle * 2 <= chips:
        middle *= 2
    if chips % middle:
        middle = 1
    return chips // middle, middle


def kernel(
    count, height, width,
    image_in, var_in, zp_in, mask_in, owner_in, stamp_in,
    diff_ref, inv_ref, coef_ref,
    x1, x2, g1, g2, ra1, ra2, rb1, rb2, rc1, rc2,
    s_own, s_mid, s_sum, sa, sb, sc,
    lhs, across, bases, onehot, design,
    image_ref, var_ref, zp_ref, mask_ref, owner_ref, stamp_ref, load,
    send1, recv1, send2, recv2, send3, recv3,
):
    zn, yn_count = grid_of(count)
    half = zn * yn_count
    _, pr, pcc = x1.shape
    subs = width // pcc
    groups = height // pr
    npix = stamp_ref.shape[1]

    me = lax.axis_index("epoch")
    core = lax.rem(me, 2)
    chip = me // 2
    y = lax.rem(chip, yn_count)
    z = chip // yn_count

    def device(zz, yy, cc):
        return {"epoch": (zz * yn_count + yy) * 2 + cc}

    def flip(value, m):
        bit = 1
        while bit <= m:
            if m & bit:
                value = value + bit * (1 - 2 * lax.rem(value // bit, 2))
            bit *= 2
        return value

    mate = device(z, y, 1 - core)
    ys = [flip(y, e) for e in range(1, yn_count)]
    zs = [flip(z, m) for m in range(1, zn)]
    peers = [mate] + [device(z, yy, core) for yy in ys] + [device(zz, y, core) for zz in zs]
    mine = (core * yn_count + y) * zn + z

    barrier = pltpu.get_barrier_semaphore()
    for peer in peers:
        pl.semaphore_signal(barrier, inc=1, device_id=peer, device_id_type=MESH)

    loads = [
        pltpu.make_async_copy(src, dst, load.at[i])
        for i, (src, dst) in enumerate((
            (image_in, image_ref), (var_in, var_ref), (mask_in, mask_ref),
            (zp_in, zp_ref), (owner_in, owner_ref), (stamp_in, stamp_ref),
        ))
    ]
    for copy in loads:
        copy.start()

    pending = []

    class Lane:
        def __init__(self, send, recv):
            self.send, self.recv, self.next = send, recv, 0

        def start(self, src, dst, device_id):
            copy = pltpu.make_async_remote_copy(
                src_ref=src, dst_ref=dst, send_sem=self.send.at[self.next], recv_sem=self.recv.at[self.next],
                device_id=device_id, device_id_type=MESH,
            )
            self.next += 1
            copy.start()
            pending.append(copy)
            return copy

    order = list(range(zn - 1, -1, -1))

    class Reduce:
        def __init__(self, x, g, ra, rb, rc, lane):
            self.x, self.g, self.ra, self.rb, self.rc, self.lane = x, g, ra, rb, rc, lane
            self.at = {}

        def a(self):
            for m in order:
                zz = flip(z, m)
                for e in list(range(1, yn_count)) + [0]:
                    src = flip(y, e) * zn + zz
                    self.at["a", e, m] = self.lane.start(
                        self.x.at[(1 - core) * half + src], self.ra.at[src], mate
                    )

        def b(self, m):
            zz = flip(z, m)
            for e in range(1, yn_count):
                yy = flip(y, e)
                own = core * half + yy * zn + zz
                self.at["a", e, m].wait_recv()
                self.x[own] = self.x[own] + self.ra[yy * zn + zz]
                self.at["b", e, m] = self.lane.start(self.x.at[own], self.rb.at[e - 1, zz], device(z, yy, core))

        def c(self, m):
            zz = flip(z, m)
            own = core * half + y * zn + zz
            self.at["a", 0, m].wait_recv()
            total = self.x[own] + self.ra[y * zn + zz]
            for e in range(1, yn_count):
                self.at["b", e, m].wait_recv()
                total = total + self.rb[e - 1, zz]
            self.x[own] = total
            if m:
                self.at["c", m] = self.lane.start(self.x.at[own], self.rc.at[m - 1], device(zz, y, core))

        def d(self, final):
            total = self.x[mine]
            for m in order[::-1]:
                if m:
                    self.at["c", m].wait_recv()
                    total = total + self.rc[m - 1]
            self.g[mine] = final(total)
            for m in order:
                if m:
                    self.at["d", m] = self.lane.start(
                        self.g.at[mine], self.g.at[mine], device(flip(z, m), y, core)
                    )
            self.forward(0)

        def forward(self, m):
            if m:
                self.at["d", m].wait_recv()
            block = self.g.at[(core * yn_count + y) * zn + flip(z, m)]
            for e in range(1, yn_count):
                self.at["e", e, m] = self.lane.start(block, block, device(z, flip(y, e), core))
            self.at["f", 0, m] = self.lane.start(block, block, mate)

        def mate_on(self, m):
            for e in range(1, yn_count):
                self.at["e", e, m].wait_recv()
                block = self.g.at[(core * yn_count + flip(y, e)) * zn + flip(z, m)]
                self.at["f", e, m] = self.lane.start(block, block, mate)

        def end(self):
            for m in order[::-1]:
                for e in range(yn_count):
                    self.at["f", e, m].wait_recv()

    def group(ref, gi):
        parts = [ref[gi * subs + s] for s in range(subs)]
        return parts[0] if subs == 1 else jnp.concatenate(parts, axis=1)

    def put_group(ref, gi, value):
        for s in range(subs):
            ref[gi * subs + s] = value[:, s * pcc:(s + 1) * pcc]

    one = Reduce(x1, g1, ra1, rb1, rc1, Lane(send1, recv1))
    two = Reduce(x2, g2, ra2, rb2, rc2, Lane(send2, recv2))
    tiny = Lane(send3, recv3)

    for copy in loads:
        copy.wait()
    weight = 1.0 / jnp.full((8, LANES), var_ref[0], jnp.float32)
    mask = jnp.full((8, LANES), mask_ref[0, 0].astype(jnp.float32), jnp.float32)
    block_term = weight * mask
    term = block_term[0:1, 0:1]
    lane = lax.broadcasted_iota(jnp.int32, (8, LANES), 1)
    small = jnp.where(lane == TILES, block_term, 0.0)
    for t in range(TILES):
        value = jnp.where(owner_ref[t] == me, zp_ref[0], 0.0)
        small = small + jnp.where(lane == t, value, 0.0)
    s_own[...] = small
    for gi in range(groups):
        put_group(x1, gi, image_ref[0, gi * pr:(gi + 1) * pr, :] * term)

    pl.semaphore_wait(barrier, len(peers))
    tiny_a = [tiny.start(s_own, sa, mate)]
    one.a()

    sharp = image_ref[0].astype(jnp.bfloat16)
    ntile = width // LANES
    zero = jnp.zeros((height, LANES), jnp.bfloat16)
    for t in range(ntile):
        for s in range(3):
            src = t + s - 1
            value = sharp[:, src * LANES:(src + 1) * LANES] if 0 <= src < ntile else zero
            lhs[t * height:(t + 1) * height, s * LANES:(s + 1) * LANES] = value
    off_h = (
        lax.broadcasted_iota(jnp.int32, (3 * LANES, LANES), 0)
        - LANES
        - lax.broadcasted_iota(jnp.int32, (3 * LANES, LANES), 1)
    ).astype(jnp.float32)
    off_v = (
        lax.broadcasted_iota(jnp.int32, (height, height), 1) - lax.broadcasted_iota(jnp.int32, (height, height), 0)
    ).astype(jnp.float32)

    def horizontal(si):
        sigma = sigma_list[si]
        band = jnp.concatenate([tap_values(off_h, sigma, degree) for degree in (0, 1, 2)], axis=1)
        for t in range(0, ntile, 2):
            res = jnp.dot(
                lhs[t * height:(t + 2) * height, :], band, preferred_element_type=jnp.float32
            ).astype(jnp.bfloat16)
            for u in range(2):
                for degree in (0, 1, 2):
                    across[si * 3 + degree, :, (t + u) * LANES:(t + u + 1) * LANES] = res[
                        u * height:(u + 1) * height, degree * LANES:(degree + 1) * LANES
                    ]

    def vertical(si):
        sigma = sigma_list[si]
        bands = [tap_values(off_v, sigma, degree) for degree in (0, 1, 2)]
        for i, j in basis_pairs:
            k = si * 4 + basis_pairs.index((i, j))
            bases[k * height:(k + 1) * height, :] = jnp.dot(
                bands[j], across[si * 3 + i], preferred_element_type=jnp.float32
            ).astype(jnp.bfloat16)

    horizontal(0)

    tiny_a[0].wait_recv()
    s_mid[...] = s_own[...] + sa[...]
    tiny_b = [tiny.start(s_mid, sb.at[d], device(z, yy, core)) for d, yy in enumerate(ys)]
    for m in order:
        one.b(m)

    horizontal(1)

    for copy in tiny_b:
        copy.wait_recv()
    total = s_mid[...]
    for d in range(yn_count - 1):
        total = total + sb[d]
    s_sum[...] = total
    tiny_c = [tiny.start(s_sum, sc.at[d], device(zz, y, core)) for d, zz in enumerate(zs)]
    for m in order:
        one.c(m)
    horizontal(2)
    for si in range(3):
        vertical(si)

    stamp = stamp_ref[...]
    shift = width.bit_length() - 1
    rows = lax.shift_right_logical(stamp, shift)
    cols = stamp - lax.shift_left(rows, shift)
    onehot[...] = jnp.where(
        lax.broadcasted_iota(jnp.int32, (width, npix), 0) == cols, 1.0, 0.0
    ).astype(jnp.bfloat16)
    row_hit = lax.broadcasted_iota(jnp.int32, (height, npix), 0) == rows
    design[...] = jnp.zeros_like(design)

    def pick(k):
        got = jnp.dot(
            bases[k * height:(k + 1) * height, :], onehot[...], preferred_element_type=jnp.float32
        )
        design[16 + k:17 + k, :] = jnp.sum(jnp.where(row_hit, got, 0.0), axis=0, keepdims=True)

    design[16 + NBASIS:17 + NBASIS, :] = jnp.ones((1, npix), jnp.float32)
    design[17 + NBASIS:18 + NBASIS, :] = 2.0 * (cols.astype(jnp.float32) + 0.5) / width - 1.0
    design[18 + NBASIS:19 + NBASIS, :] = 2.0 * (rows.astype(jnp.float32) + 0.5) / height - 1.0

    for copy in tiny_c:
        copy.wait_recv()
    total = s_sum[...]
    for d in range(zn - 1):
        total = total + sc[d]
    denom = 1.0 + total[:, TILES:TILES + 1]
    col_in = lax.broadcasted_iota(jnp.int32, (pr, pcc), 1) + lax.rem(mine, subs) * pcc

    def make_reference(numer):
        scale = jnp.broadcast_to(total[:1, 0:1], (pr, pcc))
        for t in range(1, TILES):
            scale = jnp.where(
                col_in >= t * (width // TILES), jnp.broadcast_to(total[:1, t:t + 1], (pr, pcc)), scale
            )
        return numer / jnp.broadcast_to(denom[:1], (pr, pcc)) * scale

    one.d(make_reference)
    for k in range(NBASIS // 2):
        pick(k)
    for m in range(1, zn):
        one.forward(m)
    for k in range(NBASIS // 2, NBASIS):
        pick(k)
    for m in range(zn):
        one.mate_on(m)

    rowi = lax.broadcasted_iota(jnp.int32, (16, LANES), 0)
    lanei = lax.broadcasted_iota(jnp.int32, (16, LANES), 1)
    normal = lax.dot_general(
        design[16:32, :], design[...], (((1,), (1,)), ((), ())),
        precision=lax.Precision.HIGHEST, preferred_element_type=jnp.float32,
    )
    aug = jnp.where(lanei == rowi + 16, normal + 0.05 * normal, normal)
    aug = jnp.where(lanei == rowi, 1.0, aug)
    aug = jnp.where((rowi == 15) & (lanei == 31), 1.0, aug)
    for k in range(NBASIS + 3):
        row = aug[k:k + 1, :] / aug[k:k + 1, 16 + k:17 + k]
        aug = jnp.where(rowi == k, row, aug - aug[:, 16 + k:17 + k] * row)

    mid_row = height // 2
    half_row = lax.broadcasted_iota(jnp.int32, (mid_row, npix), 0)

    def picked_of(side):
        ref_img = jnp.concatenate([group(g1, side * (groups // 2) + gi) for gi in range(groups // 2)], axis=0)
        hi = ref_img.astype(jnp.bfloat16)
        rest = ref_img - hi.astype(jnp.float32)
        mid = rest.astype(jnp.bfloat16)
        low = (rest - mid.astype(jnp.float32)).astype(jnp.bfloat16)
        got = jnp.zeros((mid_row, npix), jnp.float32)
        for part in (hi, mid, low):
            got = got + jnp.dot(part, onehot[...], preferred_element_type=jnp.float32)
        return jnp.sum(jnp.where(half_row + side * mid_row == rows, got, 0.0), axis=0, keepdims=True)

    picked = picked_of(core)
    one.end()
    picked = picked + picked_of(1 - core)
    rhs = jnp.sum(design[16:32, :] * picked, axis=1, keepdims=True)
    coef = jnp.sum(aug * rhs, axis=0, keepdims=True)
    coef_ref[...] = coef[:, 0:NBASIS + 3]

    mask_one = mask[0:1, 0:1]
    span = 16
    xn = 2.0 * (lax.broadcasted_iota(jnp.int32, (1, width), 1).astype(jnp.float32) + 0.5) / width - 1.0
    across_x = coef[:, NBASIS:NBASIS + 1] + coef[:, NBASIS + 1:NBASIS + 2] * xn
    coefs = [coef[:, k:k + 1] for k in range(NBASIS + 3)]
    for r0 in range(0, height, span):
        side = 1 - core if r0 < mid_row else core
        if r0 == mid_row:
            two.a()
        row = pl.multiple_of(side * mid_row + r0 % mid_row, span)
        model = jnp.zeros((span, width), jnp.float32)
        for k in range(NBASIS):
            model = model + coefs[k] * bases[pl.ds(k * height + row, span), :].astype(jnp.float32)
        ynv = 2.0 * ((lax.broadcasted_iota(jnp.int32, (span, 1), 0) + row).astype(jnp.float32) + 0.5) / height - 1.0
        model = model + across_x + coefs[NBASIS + 2] * ynv
        for q in range(span // pr):
            gi = row // pr + q
            diff = mask_one * (model[q * pr:(q + 1) * pr, :] - group(g1, gi))
            diff_ref[pl.ds(pl.multiple_of(row + q * pr, pr), pr), :] = diff
            put_group(x2, gi, diff * diff)
    for m in order:
        two.b(m)
    for m in order:
        two.c(m)
    two.d(lambda pooled: 1.0 / jnp.sqrt(0.05 + pooled / count))
    for m in range(1, zn):
        two.forward(m)
    for m in range(zn):
        two.mate_on(m)
    two.end()
    for gi in range(groups):
        inv_ref[gi * pr:(gi + 1) * pr, :] = group(g2, gi)
    for copy in pending:
        copy.wait_send()


def finish(diff_ref, inv_ref, coef_in, out_ref, coef_ref):
    out_ref[0] = diff_ref[...] * inv_ref[...]
    coef_ref[...] = coef_in[...]


def shards(images, variance, zero_point, block_mask, stamps, owners):
    _, height, width = images.shape
    count = lax.axis_size("epoch")
    npix = stamps.shape[1]
    zn, yn_count = grid_of(count)
    half = zn * yn_count
    pr = max(8, height // count)
    subs = count * pr // height
    pcc = width // subs
    f32 = jnp.float32
    big = pltpu.VMEM((count, pr, pcc), f32)
    ra = pltpu.VMEM((half, pr, pcc), f32)
    rb = pltpu.VMEM((max(1, yn_count - 1), zn, pr, pcc), f32)
    rc = pltpu.VMEM((max(1, zn - 1), pr, pcc), f32)
    tile = pltpu.VMEM((8, LANES), f32)
    nsem = 2 * (half + (yn_count - 1) * zn + (zn - 1))
    nsmall = 1 + (yn_count - 1) + (zn - 1)
    dma = pltpu.SemaphoreType.DMA
    vmem = pl.BlockSpec(memory_space=pltpu.VMEM)
    diff, inv, coef = pl.pallas_call(
        functools.partial(kernel, count, height, width),
        out_shape=(
            jax.ShapeDtypeStruct((height, width), f32),
            jax.ShapeDtypeStruct((height, width), f32),
            jax.ShapeDtypeStruct((1, NBASIS + 3), f32),
        ),
        in_specs=[pl.BlockSpec(memory_space=pltpu.HBM)] * 6,
        out_specs=(vmem,) * 3,
        scratch_shapes=[
            big, big, big, big, ra, ra, rb, rb, rc, rc,
            tile, tile, tile, tile,
            pltpu.VMEM((max(1, yn_count - 1), 8, LANES), f32),
            pltpu.VMEM((max(1, zn - 1), 8, LANES), f32),
            pltpu.VMEM((width // LANES * height, 3 * LANES), jnp.bfloat16),
            pltpu.VMEM((9, height, width), jnp.bfloat16),
            pltpu.VMEM((NBASIS * height, width), jnp.bfloat16),
            pltpu.VMEM((width, npix), jnp.bfloat16),
            pltpu.VMEM((LANES, npix), f32),
            pltpu.VMEM(images.shape, f32),
            pltpu.SMEM((1,), f32), pltpu.SMEM((1,), f32),
            pltpu.SMEM(block_mask.shape, jnp.int32), pltpu.SMEM(owners.shape, jnp.int32),
            pltpu.VMEM(stamps.shape, jnp.int32), dma((6,)),
            dma((nsem,)), dma((nsem,)), dma((nsem,)), dma((nsem,)), dma((nsmall,)), dma((nsmall,)),
        ],
        compiler_params=pltpu.CompilerParams(
            collective_id=0, has_side_effects=True, vmem_limit_bytes=40 * 1024 * 1024
        ),
    )(images, variance, zero_point, block_mask, owners, stamps)
    return pl.pallas_call(
        finish,
        out_shape=(
            jax.ShapeDtypeStruct(images.shape, f32),
            jax.ShapeDtypeStruct((1, NBASIS + 3), f32),
        ),
        in_specs=[vmem] * 3,
        out_specs=(vmem,) * 2,
        compiler_params=pltpu.CompilerParams(vmem_limit_bytes=8 * 1024 * 1024),
    )(diff, inv, coef)


def solution(mesh):
    in_specs = (
        P(("patch", "epoch"), None, None),
        P(("patch", "epoch")),
        P(("patch", "epoch")),
        P(("patch", "epoch"), None),
        P(("patch", "epoch"), None),
        P("patch"),
    )
    out_specs = (P(("patch", "epoch"), None, None), P(("patch", "epoch"), None))
    return jax.shard_map(shards, mesh=mesh, in_specs=in_specs, out_specs=out_specs, check_vma=False)
```

profile of v0, /device:TPU:0, one launch (start us, length us, event | category | flops | bytes accessed | tf_op | source)
XLA Modules:
  0.0 47.5 jit_solution(16042504168075938874)
XLA Ops:
  1.3 0.0 copy-start.1
  1.9 0.0 copy-start.2
  2.6 0.0 copy-done.1
  2.6 0.0 copy-done.2
  2.6 0.0 copy-start
  2.6 1.0 %copy-done = f32[1,128,1024]{2,1,0:T(8,128)S(1)} copy-done((f32[1,128,1024]{2,1,0:T(8,128)S(1)}, f32[1,128,1024]{2,1,0:T(8,128)}, u32[]{:S(2)}) %copy-start) | copy-done | bytes 524312
  3.7 43.0 %shard_map.77 = (f32[128,1024]{1,0:T(8,128)S(1)}, f32[128,1024]{1,0:T(8,128)S(1)}, f32[1,15]{1,0:T(1,128)S(1)}) custom-call(f32[1,128,1024]{2,1,0:T(8,128)S(1)} %copy-done, f32[1]{0:T(128)S(6)} %copy.8.var_in, f32[1]{0:T(128)S(6)} %copy.9.zp_in, s32[1,1]{1,0:T(1,128)S(6)} %copy.10.mask_in, s32[4]{0:T(128)S(1)} %copy-done.2, s32[1,512]{1,0:T(1,128)S(1)} %copy-done.1), custom_call_target="tpu_custom_call" | custom-call | tf_op jit(solution)/shard_map/pallas_call | solution.py:413
  46.7 0.9 %shard_map.78 = (f32[1,128,1024]{2,1,0:T(8,128)}, f32[1,15]{1,0:T(1,128)}) custom-call(f32[128,1024]{1,0:T(8,128)S(1)} %get-tuple-element.5.diff_ref, f32[128,1024]{1,0:T(8,128)S(1)} %get-tuple-element.6.inv_ref, f32[1,15]{1,0:T(1,128)S(1)} %get-tuple-element.7.coef_in), custom_call_target="tpu_custom_call" | custom-call | tf_op jit(solution)/shard_map/pallas_call | solution.py:442
Async XLA Ops:
  1.3 1.3 %copy-start.1 = (s32[1,512]{1,0:T(1,128)S(1)}, s32[1,512]{1,0:T(1,128)}, u32[]{:S(2)}) copy-start(s32[1,512]{1,0:T(1,128)} %stamp_in.1) | copy-start | bytes 6148
  1.9 0.7 %copy-start.2 = (s32[4]{0:T(128)S(1)}, s32[4]{0:T(128)}, u32[]{:S(2)}) copy-start(s32[4]{0:T(128)} %owner_in.1) | copy-start | bytes 52
  2.6 1.0 %copy-start = (f32[1,128,1024]{2,1,0:T(8,128)S(1)}, f32[1,128,1024]{2,1,0:T(8,128)}, u32[]{:S(2)}) copy-start(f32[1,128,1024]{2,1,0:T(8,128)} %image_in.1) | copy-start | bytes 1572868
where the time goes:
time: 47.7 us; the launch traced here: 47.5 us
  Pallas kernels  43.9 us (92%)
  between operations  2.64 us (6%)
  local copies, waits for them, and re-layouts  1.04 us (2%)
    pallas_call x1, Pallas kernels, shards(): pl.pallas_call(functools.partial(kernel, count, height, width), out_shape...  43 us
    unnamed x6, local copies, waits for them, and re-layouts  1.04 us

commit v1 on v0

v1 whole, which is shorter than its diff:
```python
import functools
import math

import jax
import jax.numpy as jnp
from jax import lax
from jax.experimental import pallas as pl
from jax.experimental.pallas import tpu as pltpu
from jax.sharding import PartitionSpec as P

TILES = 4
KHALF = 7
NBASIS = 12
LANES = 128

sigma_list = (0.75, 1.5, 3.0)
basis_pairs = ((0, 0), (2, 0), (0, 2), (1, 1))
MESH = pl.DeviceIdType.MESH


def tap_values(offset, sigma, degree):
    scaled = offset / sigma
    power = jnp.ones_like(scaled)
    for _ in range(degree):
        power = power * scaled
    value = jnp.exp(-0.5 * scaled * scaled) * power / (math.sqrt(2.0 * math.pi) * sigma)
    return jnp.where(jnp.abs(offset) <= KHALF, value, 0.0).astype(jnp.bfloat16)


def kernel(
    count, height, width, stripes,
    image_in, var_ref, zp_ref, mask_ref, owner_in, stamp_in,
    diff_ref, inv_ref, coef_ref,
    x1, x2, g1, g2, ra1, ra2, rd1, rd2,
    s_own, s_mid, sa, sd,
    lhs, across, bases, onehot, design, hits,
    image_ref, owner_ref, stamp_ref, load,
    send1, recv1, send2, recv2, send3, recv3,
):
    chips = count // 2
    _, pr, pc = x1.shape
    subs = width // (pc * stripes)
    pcc = pc * stripes
    npix = stamp_ref.shape[1]
    half_rows = height // 2

    me = lax.axis_index("epoch")
    core = lax.rem(me, 2)
    chip = me // 2
    power = chips & (chips - 1) == 0

    def device(which, cc):
        return {"epoch": which * 2 + cc}

    def to(j):
        if not power:
            return lax.rem(chip + j, chips)
        value, bit = chip, 1
        while bit <= j:
            if j & bit:
                value = value + bit * (1 - 2 * lax.rem(chip // bit, 2))
            bit *= 2
        return value

    def source(j):
        return to(j) if power else lax.rem(chip - j + chips, chips)

    order = list(range(chips - 1, 0, -1))
    mate = device(chip, 1 - core)
    peers = [mate] + [device(to(j), core) for j in order]

    barrier = pltpu.get_barrier_semaphore()
    for peer in peers:
        pl.semaphore_signal(barrier, inc=1, device_id=peer, device_id_type=MESH)

    loads = [
        pltpu.make_async_copy(src, dst, load.at[i])
        for i, (src, dst) in enumerate(((image_in, image_ref), (owner_in, owner_ref), (stamp_in, stamp_ref)))
    ]
    for copy in loads:
        copy.start()

    pending = []

    class Lane:
        def __init__(self, send, recv):
            self.send, self.recv, self.next = send, recv, 0

        def start(self, src, dst, device_id):
            copy = pltpu.make_async_remote_copy(
                src_ref=src, dst_ref=dst, send_sem=self.send.at[self.next], recv_sem=self.recv.at[self.next],
                device_id=device_id, device_id_type=MESH,
            )
            self.next += 1
            copy.start()
            pending.append(copy)
            return copy

    def first(s, side):
        return (s * 2 + side) * chips

    class Reduce:
        def __init__(self, x, g, ra, rd, lane):
            self.x, self.g, self.ra, self.rd, self.lane = x, g, ra, rd, lane
            self.at = {}

        def swap(self, s):
            self.at["a", s] = self.lane.start(
                self.x.at[pl.ds(first(s, 1 - core), chips)], self.ra.at[pl.ds(s * chips, chips)], mate
            )

        def scatter(self, s):
            self.at["a", s].wait_recv()
            for j in order:
                dest = to(j)
                own = first(s, core) + dest
                self.x[own] = self.x[own] + self.ra[s * chips + dest]
                self.at["b", s, j] = self.lane.start(
                    self.x.at[own], self.rd.at[s * chips + j], device(dest, core)
                )

        def settle(self, s, final):
            own = first(s, core) + chip
            total = self.x[own] + self.ra[s * chips + chip]
            for j in order[::-1]:
                self.at["b", s, j].wait_recv()
                total = total + self.rd[s * chips + j]
            self.g[own] = final(s, total)
            for j in order:
                self.at["d", s, j] = self.lane.start(self.g.at[own], self.g.at[own], device(to(j), core))
            self.at["e", s, 0] = self.lane.start(self.g.at[own], self.g.at[own], mate)

        def hand(self, s):
            for j in order[::-1]:
                self.at["d", s, j].wait_recv()
                block = self.g.at[first(s, core) + source(j)]
                self.at["e", s, j] = self.lane.start(block, block, mate)

        def end(self, s):
            for j in range(chips):
                self.at["e", s, j].wait_recv()

    def columns(s, sub):
        return sub * pcc + s * pc

    def piece(s, gi, sub):
        return 2 * chips * s + gi * subs + sub

    one = Reduce(x1, g1, ra1, rd1, Lane(send1, recv1))
    two = Reduce(x2, g2, ra2, rd2, Lane(send2, recv2))
    tiny = Lane(send3, recv3)

    weight = 1.0 / jnp.full((8, LANES), var_ref[0], jnp.float32)
    mask = jnp.full((8, LANES), mask_ref[0, 0].astype(jnp.float32), jnp.float32)
    block_term = weight * mask
    term = block_term[0:1, 0:1]
    lane = lax.broadcasted_iota(jnp.int32, (8, LANES), 1)
    loads[1].wait()
    small = jnp.where(lane == TILES, block_term, 0.0)
    for t in range(TILES):
        value = jnp.where(owner_ref[t] == me, zp_ref[0], 0.0)
        small = small + jnp.where(lane == t, value, 0.0)
    s_own[...] = small
    loads[0].wait()
    for s in range(stripes):
        for gi in range(height // pr):
            for sub in range(subs):
                c0 = columns(s, sub)
                x1[piece(s, gi, sub)] = image_ref[0, gi * pr:(gi + 1) * pr, c0:c0 + pc] * term

    pl.semaphore_wait(barrier, len(peers))
    tiny_a = tiny.start(s_own, sa, mate)
    for s in range(stripes):
        one.swap(s)

    sharp = image_ref[0].astype(jnp.bfloat16)
    ntile = width // LANES
    zero = jnp.zeros((height, LANES), jnp.bfloat16)

    def spread():
        for t in range(ntile):
            for s in range(3):
                src = t + s - 1
                value = sharp[:, src * LANES:(src + 1) * LANES] if 0 <= src < ntile else zero
                lhs[t * height:(t + 1) * height, s * LANES:(s + 1) * LANES] = value

    off_h = (
        lax.broadcasted_iota(jnp.int32, (3 * LANES, LANES), 0)
        - LANES
        - lax.broadcasted_iota(jnp.int32, (3 * LANES, LANES), 1)
    ).astype(jnp.float32)
    off_v = (
        lax.broadcasted_iota(jnp.int32, (height, height), 1) - lax.broadcasted_iota(jnp.int32, (height, height), 0)
    ).astype(jnp.float32)

    def horizontal(si):
        sigma = sigma_list[si]
        band = jnp.concatenate([tap_values(off_h, sigma, degree) for degree in (0, 1, 2)], axis=1)
        for t in range(0, ntile, 2):
            res = jnp.dot(
                lhs[t * height:(t + 2) * height, :], band, preferred_element_type=jnp.float32
            ).astype(jnp.bfloat16)
            for u in range(2):
                for degree in (0, 1, 2):
                    across[si * 3 + degree, :, (t + u) * LANES:(t + u + 1) * LANES] = res[
                        u * height:(u + 1) * height, degree * LANES:(degree + 1) * LANES
                    ]

    def vertical(si):
        sigma = sigma_list[si]
        bands = [tap_values(off_v, sigma, degree) for degree in (0, 1, 2)]
        for i, j in basis_pairs:
            k = si * 4 + basis_pairs.index((i, j))
            bases[k * height:(k + 1) * height, :] = jnp.dot(
                bands[j], across[si * 3 + i], preferred_element_type=jnp.float32
            ).astype(jnp.bfloat16)

    state = {}

    def stamped():
        loads[2].wait()
        stamp = stamp_ref[...]
        shift = width.bit_length() - 1
        rows = lax.shift_right_logical(stamp, shift)
        cols = stamp - lax.shift_left(rows, shift)
        onehot[...] = jnp.where(
            lax.broadcasted_iota(jnp.int32, (width, npix), 0) == cols, 1.0, 0.0
        ).astype(jnp.bfloat16)
        row_hit = lax.broadcasted_iota(jnp.int32, (height, npix), 0) == rows
        state["hit"] = row_hit
        hits[...] = lax.dot_general(
            jnp.where(row_hit, 1.0, 0.0).astype(jnp.bfloat16), onehot[...], (((1,), (1,)), ((), ())),
            preferred_element_type=jnp.float32,
        )
        design[...] = jnp.zeros_like(design)
        design[16 + NBASIS:17 + NBASIS, :] = jnp.ones((1, npix), jnp.float32)
        design[17 + NBASIS:18 + NBASIS, :] = 2.0 * (cols.astype(jnp.float32) + 0.5) / width - 1.0
        design[18 + NBASIS:19 + NBASIS, :] = 2.0 * (rows.astype(jnp.float32) + 0.5) / height - 1.0

    def pick(k):
        got = jnp.dot(
            bases[k * height:(k + 1) * height, :], onehot[...], preferred_element_type=jnp.float32
        )
        design[16 + k:17 + k, :] = jnp.sum(jnp.where(state["hit"], got, 0.0), axis=0, keepdims=True)

    def invert():
        rowi = lax.broadcasted_iota(jnp.int32, (16, LANES), 0)
        lanei = lax.broadcasted_iota(jnp.int32, (16, LANES), 1)
        normal = lax.dot_general(
            design[16:32, :], design[...], (((1,), (1,)), ((), ())),
            precision=lax.Precision.HIGHEST, preferred_element_type=jnp.float32,
        )
        aug = jnp.where(lanei == rowi + 16, normal + 0.05 * normal, normal)
        aug = jnp.where(lanei == rowi, 1.0, aug)
        aug = jnp.where((rowi == 15) & (lanei == 31), 1.0, aug)
        for k in range(NBASIS + 3):
            row = aug[k:k + 1, :] / aug[k:k + 1, 16 + k:17 + k]
            aug = jnp.where(rowi == k, row, aug - aug[:, 16 + k:17 + k] * row)
        state["aug"] = aug

    def sums():
        for copy in tiny_b:
            copy.wait_recv()
        total = s_mid[...]
        for j in order:
            total = total + sd[j]
        state["denom"] = 1.0 + total[:, TILES:TILES + 1]
        state["total"] = total

    def make_reference(s, numer):
        total = state["total"]
        col = lax.broadcasted_iota(jnp.int32, (pr, pc), 1) + s * pc
        if subs > 1:
            col = col + lax.rem(core * chips + chip, subs) * pcc
        scale = jnp.broadcast_to(total[:1, 0:1], (pr, pc))
        for t in range(1, TILES):
            scale = jnp.where(
                col >= t * (width // TILES), jnp.broadcast_to(total[:1, t:t + 1], (pr, pc)), scale
            )
        return numer / jnp.broadcast_to(state["denom"][:1], (pr, pc)) * scale

    xn = 2.0 * (lax.broadcasted_iota(jnp.int32, (1, width), 1).astype(jnp.float32) + 0.5) / width - 1.0
    span = max(16, pr)

    def xn_of(c0):
        return 2.0 * ((lax.broadcasted_iota(jnp.int32, (1, pc), 1) + c0).astype(jnp.float32) + 0.5) / width - 1.0

    def yn_of(row):
        return 2.0 * ((lax.broadcasted_iota(jnp.int32, (span, 1), 0) + row).astype(jnp.float32) + 0.5) / height - 1.0

    def fold(value):
        total = value[0:8, 0:LANES]
        for r in range(0, value.shape[0], 8):
            for c in range(0, value.shape[1], LANES):
                if r or c:
                    total = total + value[r:r + 8, c:c + LANES]
        return total

    def patch(ref, s, r0, sub):
        rows = [ref[piece(s, r0 // pr + q, sub)] for q in range(span // pr)]
        return rows[0] if len(rows) == 1 else jnp.concatenate(rows, axis=0)

    acc = [jnp.zeros((8, LANES), jnp.float32) for _ in range(NBASIS + 3)]

    def project(s):
        for r0 in range(0, height, span):
            for sub in range(subs):
                c0 = columns(s, sub)
                part = patch(g1, s, r0, sub) * hits[r0:r0 + span, c0:c0 + pc]
                for k in range(NBASIS):
                    base = bases[k * height + r0:k * height + r0 + span, c0:c0 + pc].astype(jnp.float32)
                    acc[k] = acc[k] + fold(part * base)
                acc[NBASIS] = acc[NBASIS] + fold(part)
                acc[NBASIS + 1] = acc[NBASIS + 1] + fold(part * xn_of(c0))
                acc[NBASIS + 2] = acc[NBASIS + 2] + fold(part * yn_of(r0))

    def solve():
        rows = [jnp.sum(value, axis=0, keepdims=True) for value in acc]
        rows.append(jnp.zeros((1, LANES), jnp.float32))
        rhs = jnp.sum(jnp.concatenate(rows, axis=0), axis=1, keepdims=True)
        coef = jnp.sum(state["aug"] * rhs, axis=0, keepdims=True)
        coef_ref[...] = coef[:, 0:NBASIS + 3]
        state["coefs"] = [coef[:, k:k + 1] for k in range(NBASIS + 3)]

    mask_one = mask[0:1, 0:1]

    def residual(s, side):
        coefs = state["coefs"]
        for r0 in range(0, half_rows, span):
            row = pl.multiple_of(side * half_rows + r0, span)
            for sub in range(subs):
                c0 = columns(s, sub)
                model = coefs[NBASIS] + coefs[NBASIS + 1] * xn_of(c0) + coefs[NBASIS + 2] * yn_of(row)
                for k in range(NBASIS):
                    model = model + coefs[k] * bases[
                        pl.ds(pl.multiple_of(k * height + row, span), span), c0:c0 + pc
                    ].astype(jnp.float32)
                for q in range(span // pr):
                    at = piece(s, row // pr + q, sub)
                    diff = mask_one * (model[q * pr:(q + 1) * pr, :] - g1[at])
                    diff_ref[pl.ds(pl.multiple_of(row + q * pr, pr), pr), c0:c0 + pc] = diff
                    x2[at] = diff * diff

    def root(s, pooled):
        return 1.0 / jnp.sqrt(0.05 + pooled / count)

    spread()
    horizontal(0)
    tiny_a.wait_recv()
    s_mid[...] = s_own[...] + sa[...]
    tiny_b = [tiny.start(s_mid, sd.at[j], device(to(j), core)) for j in order]
    for s in range(stripes):
        one.scatter(s)
    horizontal(1)
    horizontal(2)
    for si in range(3):
        vertical(si)
    stamped()
    sums()
    for s in range(stripes):
        one.settle(s, make_reference)
        for k in range(s * NBASIS // stripes, (s + 1) * NBASIS // stripes):
            pick(k)
    invert()
    for s in range(stripes):
        one.hand(s)
    for s in range(stripes):
        one.end(s)
        project(s)
    solve()
    for s in range(stripes):
        residual(s, 1 - core)
        two.swap(s)
    for s in range(stripes):
        residual(s, core)
        two.scatter(s)
    for s in range(stripes):
        two.settle(s, root)
    for s in range(stripes):
        two.hand(s)
    for s in range(stripes):
        two.end(s)
        for gi in range(height // pr):
            for sub in range(subs):
                c0 = columns(s, sub)
                inv_ref[gi * pr:(gi + 1) * pr, c0:c0 + pc] = g2[piece(s, gi, sub)]
    for copy in pending:
        copy.wait_send()


def finish(diff_ref, inv_ref, coef_in, out_ref, coef_ref):
    out_ref[0] = diff_ref[...] * inv_ref[...]
    coef_ref[...] = coef_in[...]


def shards(images, variance, zero_point, block_mask, stamps, owners):
    _, height, width = images.shape
    count = lax.axis_size("epoch")
    chips = count // 2
    npix = stamps.shape[1]
    pr = max(8, height // count)
    pcc = width * height // (count * pr)
    stripes = 1
    while stripes < 2 and pcc // (stripes * 2) % LANES == 0:
        stripes *= 2
    pc = pcc // stripes
    f32 = jnp.float32
    big = pltpu.VMEM((stripes * count, pr, pc), f32)
    part = pltpu.VMEM((stripes * chips, pr, pc), f32)
    tile = pltpu.VMEM((8, LANES), f32)
    nsem = stripes * (1 + 2 * (chips - 1) + chips)
    dma = pltpu.SemaphoreType.DMA
    vmem = pl.BlockSpec(memory_space=pltpu.VMEM)
    smem = pl.BlockSpec(memory_space=pltpu.SMEM)
    hbm = pl.BlockSpec(memory_space=pltpu.HBM)
    images, owners, stamps = [pltpu.with_memory_space_constraint(v, pltpu.HBM) for v in (images, owners, stamps)]
    diff, inv, coef = pl.pallas_call(
        functools.partial(kernel, count, height, width, stripes),
        out_shape=(
            jax.ShapeDtypeStruct((height, width), f32),
            jax.ShapeDtypeStruct((height, width), f32),
            jax.ShapeDtypeStruct((1, NBASIS + 3), f32),
        ),
        in_specs=[hbm, smem, smem, smem, hbm, hbm],
        out_specs=(vmem,) * 3,
        scratch_shapes=[
            big, big, big, big, part, part, part, part,
            tile, tile, tile, pltpu.VMEM((chips, 8, LANES), f32),
            pltpu.VMEM((width // LANES * height, 3 * LANES), jnp.bfloat16),
            pltpu.VMEM((9, height, width), jnp.bfloat16),
            pltpu.VMEM((NBASIS * height, width), jnp.bfloat16),
            pltpu.VMEM((width, npix), jnp.bfloat16),
            pltpu.VMEM((LANES, npix), f32),
            pltpu.VMEM((height, width), f32),
            pltpu.VMEM(images.shape, f32),
            pltpu.SMEM(owners.shape, jnp.int32),
            pltpu.VMEM(stamps.shape, jnp.int32), dma((3,)),
            dma((nsem,)), dma((nsem,)), dma((nsem,)), dma((nsem,)), dma((chips,)), dma((chips,)),
        ],
        compiler_params=pltpu.CompilerParams(
            collective_id=0, has_side_effects=True, vmem_limit_bytes=40 * 1024 * 1024
        ),
    )(images, variance, zero_point, block_mask, owners, stamps)
    return pl.pallas_call(
        finish,
        out_shape=(
            jax.ShapeDtypeStruct((1, height, width), f32),
            jax.ShapeDtypeStruct((1, NBASIS + 3), f32),
        ),
        in_specs=[vmem] * 3,
        out_specs=(vmem,) * 2,
        compiler_params=pltpu.CompilerParams(vmem_limit_bytes=8 * 1024 * 1024),
    )(diff, inv, coef)


def solution(mesh):
    in_specs = (
        P(("patch", "epoch"), None, None),
        P(("patch", "epoch")),
        P(("patch", "epoch")),
        P(("patch", "epoch"), None),
        P(("patch", "epoch"), None),
        P("patch"),
    )
    out_specs = (P(("patch", "epoch"), None, None), P(("patch", "epoch"), None))
    return jax.shard_map(shards, mesh=mesh, in_specs=in_specs, out_specs=out_specs, check_vma=False)
```

time: 47.7 us -> 43.2 us (0.906)
  Pallas kernels: 43.9 us -> 40.4 us
  local copies, waits for them, and re-layouts: 1.04 us -> 0 us
    pallas_call x2, Pallas kernels: 43.9 us -> 40.4 us  [the longest x1 39.5 us: shards(): pl.pallas_call(functools.partial(kernel, count, height, width, stripes),...]
    unnamed x6 -> x0, local copies, waits for them, and re-layouts: 1.04 us -> none
where the time goes in v1:
time: 43.2 us; the launch traced here: 43 us
  Pallas kernels  40.4 us (94%)
  between operations  2.57 us (6%)
    pallas_call x1, Pallas kernels, shards(): pl.pallas_call(functools.partial(kernel, count, height, width, stripes),...  39.5 us

profile of v1, /device:TPU:0, one launch (start us, length us, event | category | flops | bytes accessed | tf_op | source)
XLA Modules:
  0.0 43.0 jit_solution(1426270978338280348)
XLA Ops:
  2.6 39.5 %shard_map.77 = (f32[128,1024]{1,0:T(8,128)S(1)}, f32[128,1024]{1,0:T(8,128)S(1)}, f32[1,15]{1,0:T(1,128)S(1)}) custom-call(f32[1,128,1024]{2,1,0:T(8,128)} %image_in.1, f32[1]{0:T(128)S(6)} %copy.8.var_ref, f32[1]{0:T(128)S(6)} %copy.9.zp_ref, s32[1,1]{1,0:T(1,128)S(6)} %copy.10.mask_ref, s32[4]{0:T(128)} %owner_in.1, s32[1,512]{1,0:T(1,128)} %stamp_in.1), custom_call_target="tpu_custom_call" | custom-call | tf_op jit(solution)/shard_map/pallas_call | solution.py:417
  42.1 0.9 %shard_map.78 = (f32[1,128,1024]{2,1,0:T(8,128)}, f32[1,15]{1,0:T(1,128)}) custom-call(f32[128,1024]{1,0:T(8,128)S(1)} %get-tuple-element.5.diff_ref, f32[128,1024]{1,0:T(8,128)S(1)} %get-tuple-element.6.inv_ref, f32[1,15]{1,0:T(1,128)S(1)} %get-tuple-element.7.coef_in), custom_call_target="tpu_custom_call" | custom-call | tf_op jit(solution)/shard_map/pallas_call | solution.py:444

commit v2 on v1

--- a/solution.py
+++ b/solution.py
@@ -31,11 +31,11 @@
     count, height, width, stripes,
     image_in, var_ref, zp_ref, mask_ref, owner_in, stamp_in,
     diff_ref, inv_ref, coef_ref,
-    x1, x2, g1, g2, ra1, ra2, rd1, rd2,
-    s_own, s_mid, sa, sd,
+    x1, x2, g1, g2, ra1, ra2, rd1, rd2, rx1, rx2,
+    s_own, s_mid, s_near, sa, sd, sx,
     lhs, across, bases, onehot, design, hits,
     image_ref, owner_ref, stamp_ref, load,
-    send1, recv1, send2, recv2, send3, recv3,
+    send1, recv1, send2, recv2, send3, recv3, told,
 ):
     chips = count // 2
     _, pr, pc = x1.shape
@@ -47,14 +47,12 @@
     me = lax.axis_index("epoch")
     core = lax.rem(me, 2)
     chip = me // 2
-    power = chips & (chips - 1) == 0
+    near = chips // 2
 
     def device(which, cc):
         return {"epoch": which * 2 + cc}
 
     def to(j):
-        if not power:
-            return lax.rem(chip + j, chips)
         value, bit = chip, 1
         while bit <= j:
             if j & bit:
@@ -62,20 +60,48 @@
             bit *= 2
         return value
 
-    def source(j):
-        return to(j) if power else lax.rem(chip - j + chips, chips)
-
-    order = list(range(chips - 1, 0, -1))
+    order = list(range(near - 1, 0, -1))
     mate = device(chip, 1 - core)
-    peers = [mate] + [device(to(j), core) for j in order]
+    slot = lax.rem(chip, near)
 
     barrier = pltpu.get_barrier_semaphore()
-    for peer in peers:
-        pl.semaphore_signal(barrier, inc=1, device_id=peer, device_id_type=MESH)
+
+    @pl.when(core == 1)
+    def _():
+        pl.semaphore_signal(barrier, inc=1, device_id=mate, device_id_type=MESH)
+
+    for j in order + [near]:
+        pl.semaphore_signal(barrier, inc=1, device_id=device(to(j), 1), device_id_type=MESH)
+
+    def enter_mate():
+        @pl.when(core == 0)
+        def _():
+            pl.semaphore_wait(barrier, 1)
+            pl.semaphore_signal(told, inc=1, device_id=mate, device_id_type=MESH)
+
+        @pl.when(core == 1)
+        def _():
+            pl.semaphore_wait(told, 1)
+
+    def enter_chips():
+        @pl.when(core == 1)
+        def _():
+            pl.semaphore_wait(barrier, 2 * near)
+            pl.semaphore_signal(told, inc=1, device_id=mate, device_id_type=MESH)
+
+        @pl.when(core == 0)
+        def _():
+            pl.semaphore_wait(told, 1)
+
+    def half_of(side):
+        return pl.ds(pl.multiple_of(side * half_rows, 8), half_rows)
 
     loads = [
         pltpu.make_async_copy(src, dst, load.at[i])
-        for i, (src, dst) in enumerate(((image_in, image_ref), (owner_in, owner_ref), (stamp_in, stamp_ref)))
+        for i, (src, dst) in enumerate((
+            (image_in.at[0, half_of(1 - core)], image_ref.at[0, half_of(1 - core)]), (owner_in, owner_ref),
+            (image_in.at[0, half_of(core)], image_ref.at[0, half_of(core)]), (stamp_in, stamp_ref),
+        ))
     ]
     for copy in loads:
         copy.start()
@@ -97,57 +123,69 @@
             return copy
 
     def first(s, side):
-        return (s * 2 + side) * chips
+        return (s * 2 + side) * near
 
     class Reduce:
-        def __init__(self, x, g, ra, rd, lane):
-            self.x, self.g, self.ra, self.rd, self.lane = x, g, ra, rd, lane
+        def __init__(self, x, g, ra, rd, rx, lane):
+            self.x, self.g, self.ra, self.rd, self.rx, self.lane = x, g, ra, rd, rx, lane
             self.at = {}
 
         def swap(self, s):
             self.at["a", s] = self.lane.start(
-                self.x.at[pl.ds(first(s, 1 - core), chips)], self.ra.at[pl.ds(s * chips, chips)], mate
+                self.x.at[pl.ds(first(s, 1 - core), near)], self.ra.at[pl.ds(s * near, near)], mate
             )
 
+        def merge(self, s):
+            self.at["a", s].wait_recv()
+            for c in range(near):
+                own = first(s, core) + c
+                self.x[own] = self.x[own] + self.ra[s * near + c]
+
         def scatter(self, s):
-            self.at["a", s].wait_recv()
             for j in order:
-                dest = to(j)
-                own = first(s, core) + dest
-                self.x[own] = self.x[own] + self.ra[s * chips + dest]
                 self.at["b", s, j] = self.lane.start(
-                    self.x.at[own], self.rd.at[s * chips + j], device(dest, core)
+                    self.x.at[first(s, core) + lax.rem(to(j), near)], self.rd.at[s * near + j], device(to(j), core)
                 )
 
-        def settle(self, s, final):
-            own = first(s, core) + chip
-            total = self.x[own] + self.ra[s * chips + chip]
+        def cross(self, s):
+            own = first(s, core) + slot
+            total = self.x[own]
             for j in order[::-1]:
                 self.at["b", s, j].wait_recv()
-                total = total + self.rd[s * chips + j]
-            self.g[own] = final(s, total)
+                total = total + self.rd[s * near + j]
+            self.x[own] = total
+            self.at["c", s] = self.lane.start(self.x.at[own], self.rx.at[s], device(to(near), core))
+
+        def settle(self, s, final):
+            own = first(s, core) + slot
+            self.at["c", s].wait_recv()
+            self.g[own] = final(s, self.x[own] + self.rx[s])
             for j in order:
                 self.at["d", s, j] = self.lane.start(self.g.at[own], self.g.at[own], device(to(j), core))
-            self.at["e", s, 0] = self.lane.start(self.g.at[own], self.g.at[own], mate)
+            block = self.g.at[pl.ds(own, 1)]
+            self.at["e", s, 0] = self.lane.start(block, block, mate)
 
         def hand(self, s):
-            for j in order[::-1]:
+            for j in range(1, near):
                 self.at["d", s, j].wait_recv()
-                block = self.g.at[first(s, core) + source(j)]
-                self.at["e", s, j] = self.lane.start(block, block, mate)
+                if j % 2:
+                    where = lax.rem(to(j), near)
+                    start = where if j == 1 else where // 2 * 2
+                    block = self.g.at[pl.ds(first(s, core) + start, 1 if j == 1 else 2)]
+                    self.at["e", s, j] = self.lane.start(block, block, mate)
 
         def end(self, s):
-            for j in range(chips):
+            for j in [0] + list(range(1, near, 2)):
                 self.at["e", s, j].wait_recv()
 
     def columns(s, sub):
         return sub * pcc + s * pc
 
     def piece(s, gi, sub):
-        return 2 * chips * s + gi * subs + sub
-
-    one = Reduce(x1, g1, ra1, rd1, Lane(send1, recv1))
-    two = Reduce(x2, g2, ra2, rd2, Lane(send2, recv2))
+        return 2 * near * s + gi * subs + sub
+
+    one = Reduce(x1, g1, ra1, rd1, rx1, Lane(send1, recv1))
+    two = Reduce(x2, g2, ra2, rd2, rx2, Lane(send2, recv2))
     tiny = Lane(send3, recv3)
 
     weight = 1.0 / jnp.full((8, LANES), var_ref[0], jnp.float32)
@@ -161,23 +199,19 @@
         value = jnp.where(owner_ref[t] == me, zp_ref[0], 0.0)
         small = small + jnp.where(lane == t, value, 0.0)
     s_own[...] = small
-    loads[0].wait()
-    for s in range(stripes):
-        for gi in range(height // pr):
+
+    def weigh(s, side):
+        for r0 in range(0, half_rows, pr):
+            row = pl.multiple_of(side * half_rows + r0, pr)
             for sub in range(subs):
                 c0 = columns(s, sub)
-                x1[piece(s, gi, sub)] = image_ref[0, gi * pr:(gi + 1) * pr, c0:c0 + pc] * term
-
-    pl.semaphore_wait(barrier, len(peers))
-    tiny_a = tiny.start(s_own, sa, mate)
-    for s in range(stripes):
-        one.swap(s)
-
-    sharp = image_ref[0].astype(jnp.bfloat16)
+                x1[piece(s, row // pr, sub)] = image_ref[0, pl.ds(row, pr), c0:c0 + pc] * term
+
     ntile = width // LANES
     zero = jnp.zeros((height, LANES), jnp.bfloat16)
 
     def spread():
+        sharp = image_ref[0].astype(jnp.bfloat16)
         for t in range(ntile):
             for s in range(3):
                 src = t + s - 1
@@ -218,7 +252,7 @@
     state = {}
 
     def stamped():
-        loads[2].wait()
+        loads[3].wait()
         stamp = stamp_ref[...]
         shift = width.bit_length() - 1
         rows = lax.shift_right_logical(stamp, shift)
@@ -258,12 +292,16 @@
             aug = jnp.where(rowi == k, row, aug - aug[:, 16 + k:17 + k] * row)
         state["aug"] = aug
 
-    def sums():
-        for copy in tiny_b:
-            copy.wait_recv()
+    def gather_small():
         total = s_mid[...]
         for j in order:
+            tiny_b[j].wait_recv()
             total = total + sd[j]
+        s_near[...] = total
+
+    def sums():
+        tiny_c.wait_recv()
+        total = s_near[...] + sx[...]
         state["denom"] = 1.0 + total[:, TILES:TILES + 1]
         state["total"] = total
 
@@ -271,7 +309,7 @@
         total = state["total"]
         col = lax.broadcasted_iota(jnp.int32, (pr, pc), 1) + s * pc
         if subs > 1:
-            col = col + lax.rem(core * chips + chip, subs) * pcc
+            col = col + lax.rem(core * near + slot, subs) * pcc
         scale = jnp.broadcast_to(total[:1, 0:1], (pr, pc))
         for t in range(1, TILES):
             scale = jnp.where(
@@ -320,48 +358,80 @@
         rhs = jnp.sum(jnp.concatenate(rows, axis=0), axis=1, keepdims=True)
         coef = jnp.sum(state["aug"] * rhs, axis=0, keepdims=True)
         coef_ref[...] = coef[:, 0:NBASIS + 3]
-        state["coefs"] = [coef[:, k:k + 1] for k in range(NBASIS + 3)]
-
-    mask_one = mask[0:1, 0:1]
+        state["coefs"] = [jnp.broadcast_to(coef[:, k:k + 1], (span, LANES)) for k in range(NBASIS + 3)]
+
+    mask_one = jnp.broadcast_to(mask[0:1, :], (pr, LANES))
 
     def residual(s, side):
         coefs = state["coefs"]
         for r0 in range(0, half_rows, span):
             row = pl.multiple_of(side * half_rows + r0, span)
+            yterm = coefs[NBASIS] + coefs[NBASIS + 2] * yn_of(row)
             for sub in range(subs):
-                c0 = columns(s, sub)
-                model = coefs[NBASIS] + coefs[NBASIS + 1] * xn_of(c0) + coefs[NBASIS + 2] * yn_of(row)
-                for k in range(NBASIS):
-                    model = model + coefs[k] * bases[
-                        pl.ds(pl.multiple_of(k * height + row, span), span), c0:c0 + pc
-                    ].astype(jnp.float32)
-                for q in range(span // pr):
-                    at = piece(s, row // pr + q, sub)
-                    diff = mask_one * (model[q * pr:(q + 1) * pr, :] - g1[at])
-                    diff_ref[pl.ds(pl.multiple_of(row + q * pr, pr), pr), c0:c0 + pc] = diff
-                    x2[at] = diff * diff
+                for lo in range(0, pc, LANES):
+                    c0 = columns(s, sub) + lo
+                    xn = 2.0 * ((lax.broadcasted_iota(jnp.int32, (1, LANES), 1) + c0).astype(jnp.float32) + 0.5) / width - 1.0
+                    model = yterm + coefs[NBASIS + 1] * xn
+                    for k in range(NBASIS):
+                        model = model + coefs[k] * bases[
+                            pl.ds(pl.multiple_of(k * height + row, span), span), c0:c0 + LANES
+                        ].astype(jnp.float32)
+                    for q in range(span // pr):
+                        at = piece(s, row // pr + q, sub)
+                        diff = mask_one * (model[q * pr:(q + 1) * pr, :] - g1[at, :, lo:lo + LANES])
+                        diff_ref[pl.ds(pl.multiple_of(row + q * pr, pr), pr), c0:c0 + LANES] = diff
+                        x2[at, :, lo:lo + LANES] = diff * diff
 
     def root(s, pooled):
         return 1.0 / jnp.sqrt(0.05 + pooled / count)
 
+    loads[0].wait()
+    for s in range(stripes):
+        weigh(s, 1 - core)
+    enter_mate()
+    for s in range(stripes):
+        one.swap(s)
+    tiny_a = tiny.start(s_own, sa, mate)
+    loads[2].wait()
+    for s in range(stripes):
+        weigh(s, core)
     spread()
     horizontal(0)
+
+    @pl.when(chip < near)
+    def _():
+        horizontal(1)
+        horizontal(2)
+        for si in range(3):
+            vertical(si)
+
+    for s in range(stripes):
+        one.merge(s)
     tiny_a.wait_recv()
     s_mid[...] = s_own[...] + sa[...]
-    tiny_b = [tiny.start(s_mid, sd.at[j], device(to(j), core)) for j in order]
+    enter_chips()
     for s in range(stripes):
         one.scatter(s)
-    horizontal(1)
-    horizontal(2)
-    for si in range(3):
-        vertical(si)
+    tiny_b = {j: tiny.start(s_mid, sd.at[j], device(to(j), core)) for j in order}
+
+    @pl.when(chip >= near)
+    def _():
+        horizontal(1)
+        horizontal(2)
+        for si in range(3):
+            vertical(si)
+
     stamped()
+    for s in range(stripes):
+        one.cross(s)
+    gather_small()
+    tiny_c = tiny.start(s_near, sx, device(to(near), core))
+    for k in range(NBASIS):
+        pick(k)
+    invert()
     sums()
     for s in range(stripes):
         one.settle(s, make_reference)
-        for k in range(s * NBASIS // stripes, (s + 1) * NBASIS // stripes):
-            pick(k)
-    invert()
     for s in range(stripes):
         one.hand(s)
     for s in range(stripes):
@@ -373,7 +443,10 @@
         two.swap(s)
     for s in range(stripes):
         residual(s, core)
+        two.merge(s)
         two.scatter(s)
+    for s in range(stripes):
+        two.cross(s)
     for s in range(stripes):
         two.settle(s, root)
     for s in range(stripes):
@@ -398,17 +471,19 @@
     count = lax.axis_size("epoch")
     chips = count // 2
     npix = stamps.shape[1]
-    pr = max(8, height // count)
-    pcc = width * height // (count * pr)
+    near = chips // 2
+    pr = max(8, height // chips)
+    pcc = width * height // (chips * pr)
     stripes = 1
     while stripes < 2 and pcc // (stripes * 2) % LANES == 0:
         stripes *= 2
     pc = pcc // stripes
     f32 = jnp.float32
-    big = pltpu.VMEM((stripes * count, pr, pc), f32)
-    part = pltpu.VMEM((stripes * chips, pr, pc), f32)
+    big = pltpu.VMEM((stripes * chips, pr, pc), f32)
+    part = pltpu.VMEM((stripes * near, pr, pc), f32)
+    far = pltpu.VMEM((stripes, pr, pc), f32)
     tile = pltpu.VMEM((8, LANES), f32)
-    nsem = stripes * (1 + 2 * (chips - 1) + chips)
+    nsem = stripes * (2 + 2 * (near - 1) + 1 + near // 2 + 1)
     dma = pltpu.SemaphoreType.DMA
     vmem = pl.BlockSpec(memory_space=pltpu.VMEM)
     smem = pl.BlockSpec(memory_space=pltpu.SMEM)
@@ -424,8 +499,8 @@
         in_specs=[hbm, smem, smem, smem, hbm, hbm],
         out_specs=(vmem,) * 3,
         scratch_shapes=[
-            big, big, big, big, part, part, part, part,
-            tile, tile, tile, pltpu.VMEM((chips, 8, LANES), f32),
+            big, big, big, big, part, part, part, part, far, far,
+            tile, tile, tile, tile, pltpu.VMEM((near, 8, LANES), f32), tile,
             pltpu.VMEM((width // LANES * height, 3 * LANES), jnp.bfloat16),
             pltpu.VMEM((9, height, width), jnp.bfloat16),
             pltpu.VMEM((NBASIS * height, width), jnp.bfloat16),
@@ -434,8 +509,9 @@
             pltpu.VMEM((height, width), f32),
             pltpu.VMEM(images.shape, f32),
             pltpu.SMEM(owners.shape, jnp.int32),
-            pltpu.VMEM(stamps.shape, jnp.int32), dma((3,)),
-            dma((nsem,)), dma((nsem,)), dma((nsem,)), dma((nsem,)), dma((chips,)), dma((chips,)),
+            pltpu.VMEM(stamps.shape, jnp.int32), dma((4,)),
+            dma((nsem,)), dma((nsem,)), dma((nsem,)), dma((nsem,)), dma((near + 1,)), dma((near + 1,)),
+            pltpu.SemaphoreType.REGULAR,
         ],
         compiler_params=pltpu.CompilerParams(
             collective_id=0, has_side_effects=True, vmem_limit_bytes=40 * 1024 * 1024

time: 43.2 us -> 39.7 us (0.919)
  Pallas kernels: 40.4 us -> 37 us
    pallas_call x1, Pallas kernels: 39.5 us -> 36.1 us  [shards(): pl.pallas_call(functools.partial(kernel, count, height, width, stripes),...]
where the time goes in v2:
time: 39.7 us; the launch traced here: 39.6 us
  Pallas kernels  37 us (93%)
  between operations  2.57 us (6%)
    pallas_call x1, Pallas kernels, shards(): pl.pallas_call(functools.partial(kernel, count, height, width, stripes),...  36.1 us
    pallas_call x1, Pallas kernels, shards(): pl.pallas_call(finish, out_shape=(jax.ShapeDtypeStruct((1, height, width)...  0.85 us

profile of v2, /device:TPU:0, one launch (start us, length us, event | category | flops | bytes accessed | tf_op | source)
XLA Modules:
  0.0 39.6 jit_solution(16516019296222548984)
XLA Ops:
  2.6 36.1 %shard_map.77 = (f32[128,1024]{1,0:T(8,128)S(1)}, f32[128,1024]{1,0:T(8,128)S(1)}, f32[1,15]{1,0:T(1,128)S(1)}) custom-call(f32[1,128,1024]{2,1,0:T(8,128)} %image_in.1, f32[1]{0:T(128)S(6)} %copy.8.var_ref, f32[1]{0:T(128)S(6)} %copy.9.zp_ref, s32[1,1]{1,0:T(1,128)S(6)} %copy.10.mask_ref, s32[4]{0:T(128)} %owner_in.1, s32[1,512]{1,0:T(1,128)} %stamp_in.1), custom_call_target="tpu_custom_call" | custom-call | tf_op jit(solution)/shard_map/pallas_call | solution.py:492
  38.7 0.9 %shard_map.78 = (f32[1,128,1024]{2,1,0:T(8,128)}, f32[1,15]{1,0:T(1,128)}) custom-call(f32[128,1024]{1,0:T(8,128)S(1)} %get-tuple-element.5.diff_ref, f32[128,1024]{1,0:T(8,128)S(1)} %get-tuple-element.6.inv_ref, f32[1,15]{1,0:T(1,128)S(1)} %get-tuple-element.7.coef_in), custom_call_target="tpu_custom_call" | custom-call | tf_op jit(solution)/shard_map/pallas_call | solution.py:520

commit v3 on v2

--- a/solution.py
+++ b/solution.py
@@ -317,7 +317,6 @@
             )
         return numer / jnp.broadcast_to(state["denom"][:1], (pr, pc)) * scale
 
-    xn = 2.0 * (lax.broadcasted_iota(jnp.int32, (1, width), 1).astype(jnp.float32) + 0.5) / width - 1.0
     span = max(16, pr)
 
     def xn_of(c0):
@@ -398,7 +397,7 @@
     spread()
     horizontal(0)
 
-    @pl.when(chip < near)
+    @pl.when(chip < near // 2)
     def _():
         horizontal(1)
         horizontal(2)
@@ -414,7 +413,7 @@
         one.scatter(s)
     tiny_b = {j: tiny.start(s_mid, sd.at[j], device(to(j), core)) for j in order}
 
-    @pl.when(chip >= near)
+    @pl.when(chip >= near // 2)
     def _():
         horizontal(1)
         horizontal(2)
@@ -422,12 +421,12 @@
             vertical(si)
 
     stamped()
+    for k in range(NBASIS):
+        pick(k)
     for s in range(stripes):
         one.cross(s)
     gather_small()
     tiny_c = tiny.start(s_near, sx, device(to(near), core))
-    for k in range(NBASIS):
-        pick(k)
     invert()
     sums()
     for s in range(stripes):

time: 39.7 us -> 39.1 us (0.985)
  Pallas kernels: 37 us -> 36.4 us
    pallas_call x1, Pallas kernels: 36.1 us -> 35.5 us  [shards(): pl.pallas_call(functools.partial(kernel, count, height, width, stripes),...]
where the time goes in v3:
time: 39.1 us; the launch traced here: 39 us
  Pallas kernels  36.4 us (93%)
  between operations  2.57 us (7%)
    pallas_call x1, Pallas kernels, shards(): pl.pallas_call(functools.partial(kernel, count, height, width, stripes),...  35.5 us
    pallas_call x1, Pallas kernels, shards(): pl.pallas_call(finish, out_shape=(jax.ShapeDtypeStruct((1, height, width)...  0.85 us

profile of v3, /device:TPU:0, one launch (start us, length us, event | category | flops | bytes accessed | tf_op | source)
XLA Modules:
  0.0 39.0 jit_solution(3835239535449871051)
XLA Ops:
  2.6 35.5 %shard_map.77 = (f32[128,1024]{1,0:T(8,128)S(1)}, f32[128,1024]{1,0:T(8,128)S(1)}, f32[1,15]{1,0:T(1,128)S(1)}) custom-call(f32[1,128,1024]{2,1,0:T(8,128)} %image_in.1, f32[1]{0:T(128)S(6)} %copy.8.var_ref, f32[1]{0:T(128)S(6)} %copy.9.zp_ref, s32[1,1]{1,0:T(1,128)S(6)} %copy.10.mask_ref, s32[4]{0:T(128)} %owner_in.1, s32[1,512]{1,0:T(1,128)} %stamp_in.1), custom_call_target="tpu_custom_call" | custom-call | tf_op jit(solution)/shard_map/pallas_call | solution.py:491
  38.1 0.9 %shard_map.78 = (f32[1,128,1024]{2,1,0:T(8,128)}, f32[1,15]{1,0:T(1,128)}) custom-call(f32[128,1024]{1,0:T(8,128)S(1)} %get-tuple-element.5.diff_ref, f32[128,1024]{1,0:T(8,128)S(1)} %get-tuple-element.6.inv_ref, f32[1,15]{1,0:T(1,128)S(1)} %get-tuple-element.7.coef_in), custom_call_target="tpu_custom_call" | custom-call | tf_op jit(solution)/shard_map/pallas_call | solution.py:519

commit v4 on v3

--- a/solution.py
+++ b/solution.py
@@ -30,10 +30,10 @@
 def kernel(
     count, height, width, stripes,
     image_in, var_ref, zp_ref, mask_ref, owner_in, stamp_in,
-    diff_ref, inv_ref, coef_ref,
+    diff_ref, coef_ref,
     x1, x2, g1, g2, ra1, ra2, rd1, rd2, rx1, rx2,
     s_own, s_mid, s_near, sa, sd, sx,
-    lhs, across, bases, onehot, design, hits,
+    lhs, across, bases, wide, onehot, design, hits,
     image_ref, owner_ref, stamp_ref, load,
     send1, recv1, send2, recv2, send3, recv3, told,
 ):
@@ -93,14 +93,16 @@
         def _():
             pl.semaphore_wait(told, 1)
 
-    def half_of(side):
-        return pl.ds(pl.multiple_of(side * half_rows, 8), half_rows)
+    def half_of(side, part=0):
+        return pl.ds(pl.multiple_of(side * half_rows + part * (half_rows // 2), 8), half_rows // 2)
 
     loads = [
         pltpu.make_async_copy(src, dst, load.at[i])
         for i, (src, dst) in enumerate((
             (image_in.at[0, half_of(1 - core)], image_ref.at[0, half_of(1 - core)]), (owner_in, owner_ref),
             (image_in.at[0, half_of(core)], image_ref.at[0, half_of(core)]), (stamp_in, stamp_ref),
+            (image_in.at[0, half_of(1 - core, 1)], image_ref.at[0, half_of(1 - core, 1)]),
+            (image_in.at[0, half_of(core, 1)], image_ref.at[0, half_of(core, 1)]),
         ))
     ]
     for copy in loads:
@@ -317,6 +319,7 @@
             )
         return numer / jnp.broadcast_to(state["denom"][:1], (pr, pc)) * scale
 
+    xn = 2.0 * (lax.broadcasted_iota(jnp.int32, (1, width), 1).astype(jnp.float32) + 0.5) / width - 1.0
     span = max(16, pr)
 
     def xn_of(c0):
@@ -345,7 +348,7 @@
                 c0 = columns(s, sub)
                 part = patch(g1, s, r0, sub) * hits[r0:r0 + span, c0:c0 + pc]
                 for k in range(NBASIS):
-                    base = bases[k * height + r0:k * height + r0 + span, c0:c0 + pc].astype(jnp.float32)
+                    base = wide[k * height + r0:k * height + r0 + span, c0:c0 + pc]
                     acc[k] = acc[k] + fold(part * base)
                 acc[NBASIS] = acc[NBASIS] + fold(part)
                 acc[NBASIS + 1] = acc[NBASIS + 1] + fold(part * xn_of(c0))
@@ -372,9 +375,9 @@
                     xn = 2.0 * ((lax.broadcasted_iota(jnp.int32, (1, LANES), 1) + c0).astype(jnp.float32) + 0.5) / width - 1.0
                     model = yterm + coefs[NBASIS + 1] * xn
                     for k in range(NBASIS):
-                        model = model + coefs[k] * bases[
+                        model = model + coefs[k] * wide[
                             pl.ds(pl.multiple_of(k * height + row, span), span), c0:c0 + LANES
-                        ].astype(jnp.float32)
+                        ]
                     for q in range(span // pr):
                         at = piece(s, row // pr + q, sub)
                         diff = mask_one * (model[q * pr:(q + 1) * pr, :] - g1[at, :, lo:lo + LANES])
@@ -385,6 +388,7 @@
         return 1.0 / jnp.sqrt(0.05 + pooled / count)
 
     loads[0].wait()
+    loads[4].wait()
     for s in range(stripes):
         weigh(s, 1 - core)
     enter_mate()
@@ -392,6 +396,7 @@
         one.swap(s)
     tiny_a = tiny.start(s_own, sa, mate)
     loads[2].wait()
+    loads[5].wait()
     for s in range(stripes):
         weigh(s, core)
     spread()
@@ -428,6 +433,8 @@
     gather_small()
     tiny_c = tiny.start(s_near, sx, device(to(near), core))
     invert()
+    for k in range(NBASIS):
+        wide[k * height:(k + 1) * height, :] = bases[k * height:(k + 1) * height, :].astype(jnp.float32)
     sums()
     for s in range(stripes):
         one.settle(s, make_reference)
@@ -455,14 +462,23 @@
         for gi in range(height // pr):
             for sub in range(subs):
                 c0 = columns(s, sub)
-                inv_ref[gi * pr:(gi + 1) * pr, c0:c0 + pc] = g2[piece(s, gi, sub)]
+                spot = (slice(gi * pr, (gi + 1) * pr), slice(c0, c0 + pc))
+                diff_ref[spot] = diff_ref[spot] * g2[piece(s, gi, sub)]
     for copy in pending:
         copy.wait_send()
 
 
-def finish(diff_ref, inv_ref, coef_in, out_ref, coef_ref):
-    out_ref[0] = diff_ref[...] * inv_ref[...]
-    coef_ref[...] = coef_in[...]
+def finish(value_ref, coef_in, out_ref, coef_ref, sem):
+    parts = sem.shape[0] - 1
+    rows = value_ref.shape[0] // parts
+    copies = [pltpu.make_async_copy(coef_in, coef_ref, sem.at[parts])]
+    for i in range(parts):
+        spot = pl.ds(i * rows, rows)
+        copies.append(pltpu.make_async_copy(value_ref.at[spot], out_ref.at[0, spot], sem.at[i]))
+    for copy in copies:
+        copy.start()
+    for copy in copies:
+        copy.wait()
 
 
 def shards(images, variance, zero_point, block_mask, stamps, owners):
@@ -488,27 +504,27 @@
     smem = pl.BlockSpec(memory_space=pltpu.SMEM)
     hbm = pl.BlockSpec(memory_space=pltpu.HBM)
     images, owners, stamps = [pltpu.with_memory_space_constraint(v, pltpu.HBM) for v in (images, owners, stamps)]
-    diff, inv, coef = pl.pallas_call(
+    value, coef = pl.pallas_call(
         functools.partial(kernel, count, height, width, stripes),
         out_shape=(
-            jax.ShapeDtypeStruct((height, width), f32),
             jax.ShapeDtypeStruct((height, width), f32),
             jax.ShapeDtypeStruct((1, NBASIS + 3), f32),
         ),
         in_specs=[hbm, smem, smem, smem, hbm, hbm],
-        out_specs=(vmem,) * 3,
+        out_specs=(vmem,) * 2,
         scratch_shapes=[
             big, big, big, big, part, part, part, part, far, far,
             tile, tile, tile, tile, pltpu.VMEM((near, 8, LANES), f32), tile,
             pltpu.VMEM((width // LANES * height, 3 * LANES), jnp.bfloat16),
             pltpu.VMEM((9, height, width), jnp.bfloat16),
             pltpu.VMEM((NBASIS * height, width), jnp.bfloat16),
+            pltpu.VMEM((NBASIS * height, width), f32),
             pltpu.VMEM((width, npix), jnp.bfloat16),
             pltpu.VMEM((LANES, npix), f32),
             pltpu.VMEM((height, width), f32),
             pltpu.VMEM(images.shape, f32),
             pltpu.SMEM(owners.shape, jnp.int32),
-            pltpu.VMEM(stamps.shape, jnp.int32), dma((4,)),
+            pltpu.VMEM(stamps.shape, jnp.int32), dma((6,)),
             dma((nsem,)), dma((nsem,)), dma((nsem,)), dma((nsem,)), dma((near + 1,)), dma((near + 1,)),
             pltpu.SemaphoreType.REGULAR,
         ],
@@ -522,10 +538,11 @@
             jax.ShapeDtypeStruct((1, height, width), f32),
             jax.ShapeDtypeStruct((1, NBASIS + 3), f32),
         ),
-        in_specs=[vmem] * 3,
-        out_specs=(vmem,) * 2,
+        in_specs=[vmem] * 2,
+        out_specs=(hbm,) * 2,
+        scratch_shapes=[dma((9,))],
         compiler_params=pltpu.CompilerParams(vmem_limit_bytes=8 * 1024 * 1024),
-    )(diff, inv, coef)
+    )(value, coef)
 
 
 def solution(mesh):

time: 39.1 us -> 39 us (level)
  no operation moved by 1% of the time
where the time goes in v4:
time: 39 us; the launch traced here: 38.8 us
  Pallas kernels  36.2 us (93%)
  between operations  2.57 us (7%)
    pallas_call x1, Pallas kernels, shards(): pl.pallas_call(functools.partial(kernel, count, height, width, stripes),...  35.4 us
    pallas_call x1, Pallas kernels, shards(): pl.pallas_call(finish, out_shape=(jax.ShapeDtypeStruct((1, height, width)...  0.86 us

profile of v4, /device:TPU:0, one launch (start us, length us, event | category | flops | bytes accessed | tf_op | source)
XLA Modules:
  0.0 38.8 jit_solution(11470628909675069065)
XLA Ops:
  2.6 35.4 %shard_map.77 = (f32[128,1024]{1,0:T(8,128)S(1)}, f32[1,15]{1,0:T(1,128)S(1)}) custom-call(f32[1,128,1024]{2,1,0:T(8,128)} %image_in.1, f32[1]{0:T(128)S(6)} %copy.8.var_ref, f32[1]{0:T(128)S(6)} %copy.9.zp_ref, s32[1,1]{1,0:T(1,128)S(6)} %copy.10.mask_ref, s32[4]{0:T(128)} %owner_in.1, s32[1,512]{1,0:T(1,128)} %stamp_in.1), custom_call_target="tpu_custom_call" | custom-call | tf_op jit(solution)/shard_map/pallas_call | solution.py:507
  38.0 0.9 %shard_map.78 = (f32[1,128,1024]{2,1,0:T(8,128)}, f32[1,15]{1,0:T(1,128)}) custom-call(f32[128,1024]{1,0:T(8,128)S(1)} %get-tuple-element.4.value_ref, f32[1,15]{1,0:T(1,128)S(1)} %get-tuple-element.5.coef_in), custom_call_target="tpu_custom_call" | custom-call | tf_op jit(solution)/shard_map/pallas_call | solution.py:535
